TPU v7x, 128 devices: a whole 4x4x4 slice. The times are simulated.
128 devices in a mesh: seq: 16 (over z, y_hi, core), grp: 8 (over x, y_lo).
Axes of the slice: x: 4, y: 4 (y_hi: 2, y_lo: 2; y = y_hi * 2 + y_lo), z: 4, core: 2. Of those that a mesh axis runs over, the one named last changes fastest.
Arguments:
- tokens: bfloat16 [262144, 1280], P(('seq', 'grp')), may hold values from -27 to 27
- slot_keys: bfloat16 [1280, 512], replicated, may hold values from -1.5 to 1.5
- norm_gain: float32 [128, 1280], P(('seq', 'grp')), may hold values from 0.1 to 1.9
- w_in: bfloat16 [128, 1280, 2560], P(('seq', 'grp')), may hold values from -0.15625 to 0.15625
- w_out: bfloat16 [128, 2560, 1280], P(('seq', 'grp')), may hold values from -0.125 to 0.125
Outputs:
- mixed: bfloat16 [262144, 1280], P(('seq', 'grp'))
All inputs are finite; a program needn't handle non-finite values.
Results may differ from a plain program's by a relative error of at most 0.007.
Values may be sent and summed in bfloat16 or wider, within the bound.
A program may use at most 128 MiB of HBM per device.

v0:
```python
import jax
import jax.numpy as jnp
from jax import lax
from jax.sharding import PartitionSpec as P


def in_one_piece(arrays, axis, split_dim, concat_dim, along):
    columns = [a.reshape(*a.shape[:along], -1) for a in arrays]
    both = jnp.concatenate(columns, axis=along)
    out, at, finished = (
        lax.all_to_all(both, axis, split_axis=split_dim, concat_axis=concat_dim, tiled=True),
        0,
        [],
    )
    for a, column in zip(arrays, columns):
        piece = out[..., at : at + column.shape[along]]
        finished.append(piece.reshape(*piece.shape[:along], *a.shape[along:]))
        at += column.shape[along]
    return tuple(finished)


def on_device(tokens, slot_keys, norm_gain, w_in, w_out):
    devices = lax.axis_size(("seq", "grp"))
    logits = jnp.dot(tokens, slot_keys, preferred_element_type=jnp.float32)
    per_dev = logits.shape[1] // devices
    maxima = jnp.max(logits, axis=0)
    scores = jnp.exp(logits - maxima[None, :])
    totals = jnp.sum(scores, axis=0)
    weights = scores.astype(jnp.bfloat16)
    dims = (((0,), (0,)), ((), ()))
    numer_local = lax.dot_general(weights, tokens, dims, preferred_element_type=jnp.float32)
    parts, peaks, sums = in_one_piece((numer_local, maxima, totals), ("seq", "grp"), 0, 0, 1)
    peaks = peaks.reshape(devices, per_dev)
    factor = jnp.exp(peaks - jnp.max(peaks, axis=0, keepdims=True))
    numer = jnp.sum(parts.reshape(devices, per_dev, -1) * factor[:, :, None], axis=0)
    own_total = jnp.sum(sums.reshape(devices, per_dev) * factor, axis=0)
    slot_in = numer / own_total[:, None]
    normed = (slot_in * norm_gain[0][None, :]).astype(jnp.bfloat16)
    hidden = jax.nn.gelu(jnp.dot(normed, w_in[0], preferred_element_type=jnp.float32)).astype(
        jnp.bfloat16
    )
    expert_out = jnp.dot(hidden, w_out[0], preferred_element_type=jnp.float32).astype(jnp.bfloat16)
    row_top = jnp.max(logits, axis=1, keepdims=True)
    row_exp = jnp.exp(logits - row_top)
    combine = (row_exp / jnp.sum(row_exp, axis=1, keepdims=True)).astype(jnp.bfloat16)
    gathered = lax.all_gather(expert_out, ("seq", "grp"), axis=0, tiled=True)
    mixed = jnp.dot(combine, gathered, preferred_element_type=jnp.float32)
    return mixed.astype(jnp.bfloat16)


def solution(mesh):
    return jax.shard_map(
        on_device,
        mesh=mesh,
        in_specs=(
            P(("seq", "grp"), None),
            P(),
            P(("seq", "grp"), None),
            P(("seq", "grp"), None, None),
            P(("seq", "grp"), None, None),
        ),
        out_specs=P(("seq", "grp"), None),
        check_vma=False,
    )
```

profile of v0, /device:TPU:1, one launch (start us, length us, event | category | flops | bytes accessed | tf_op | source)
XLA Modules:
  0.0 423.7 jit_solution(511834206281356095)
XLA Ops:
  6.5 0.0 copy-start
  6.5 1.3 copy-done
  7.9 7.1 %fusion.44 = (f32[2048]{0:T(1024)S(1)}, f32[512]{0:T(512)S(1)}, f32[2048,512]{1,0:T(8,128)}) fusion(bf16[2048,1280]{1,0:T(8,128)(2,1)} %param.5, bf16[1280,512]{1,0:T(8,128)(2,1)S(1)} %copy-done), kind=kOutput, calls=%fused_computation.42 | convolution fusion | flops 2686449152 | bytes 10758144 | tf_op jit(solution)/shard_map/dot_general | solution.py:24
  14.9 0.3 concatenate.14
  15.3 0.0 copy-start.1
  15.3 8.4 %fusion.13 = f32[512,1280]{1,0:T(8,128)} fusion(bf16[2048,1280]{1,0:T(8,128)(2,1)} %param.5, f32[2048,512]{1,0:T(8,128)} %get-tuple-element.13, f32[512]{0:T(512)S(1)} %get-tuple-element.8), kind=kOutput, calls=%fused_computation.14 | convolution fusion | flops 2686451712 | bytes 12060672 | tf_op jit(solution)/shard_map/dot_general | solution.py:31
  23.6 0.0 copy-done.1
  23.6 1.6 fusion.4
  25.2 0.3 concatenate.15
  25.6 3.9 concatenate.10
  29.5 5.6 %concatenate.13 = f32[128,4,1282]{2,1,0:T(4,128)} concatenate(f32[128,4,1280]{2,1,0:T(4,128)} %concatenate.10, f32[128,4,1]{2,1,0:T(4,128)S(1)} %concatenate.14, f32[128,4,1]{2,1,0:T(4,128)S(1)} %concatenate.15), dimensions={2} | concatenate | bytes 5251072 | tf_op jit(solution)/shard_map/concatenate | solution.py:9
  35.1 0.0 copy-start.2
  35.1 11.9 %all-to-all-start = ((f32[128,4,1282]{2,1,0:T(4,128)}), f32[128,4,1282]{2,1,0:T(4,128)}, u32[]{:S(2)}, u32[]{:S(2)}) async-start(f32[128,4,1282]{2,1,0:T(4,128)} %concatenate.13), calls=%async_computation | async-start | bytes 5767168 | tf_op jit(solution)/shard_map/all_to_all | solution.py:11
  47.0 0.2 all-gather.3.cloned.1.call-start
  47.2 0.0 copy-done.2
  47.3 37.5 %all-to-all-done = f32[128,4,1282]{2,1,0:T(4,128)} async-done(((f32[128,4,1282]{2,1,0:T(4,128)}), f32[128,4,1282]{2,1,0:T(4,128)}, u32[]{:S(2)}, u32[]{:S(2)}) %all-to-all-start) | async-done | bytes 2625568 | tf_op jit(solution)/shard_map/all_to_all | solution.py:11
  84.8 4.4 %all_to_all.7 = f32[512,1282]{1,0:T(8,128)} reshape(f32[128,4,1282]{2,1,0:T(4,128)} %all-to-all-done) | data formatting | bytes 5251072 | tf_op jit(solution)/shard_map/all_to_all | solution.py:11
  89.2 1.3 slice_reduce_fusion
  90.5 3.4 slice.12
  93.9 3.9 reshape.37
  97.8 0.1 reshape_reshape.7
  97.9 0.1 reshape_reshape.6
  98.1 2.3 multiply_reduce_fusion
  100.5 7.3 %fusion.10 = bf16[1,4,1280]{2,1,0:T(4,128)(2,1)} fusion(bf16[1,2560,1280]{2,1,0:T(8,128)(2,1)} %param.9, bf16[1,1280,2560]{2,1,0:T(8,128)(2,1)} %param.8, f32[4,1280]{1,0:T(4,128)S(1)} %multiply_reduce_fusion, f32[1280]{0:T(1024)S(1)} %reduce.2, f32[4]{0:T(128)S(1)} %get-tuple-element.11), kind=kOutput, calls=%fused_computation.13 | convolution fusion | flops 52541440 | bytes 13143056 | tf_op jit(solution)/shard_map/dot_general | solution.py:42
  107.8 0.0 all-gather.3.cloned.1.call-update
  107.8 298.9 %all-gather.3.cloned.1.call-done = bf16[128,4,1280]{2,1,0:T(4,128)(2,1)} async-done(((bf16[1,4,1280]{2,1,0:T(4,128)(2,1)}), bf16[128,4,1280]{2,1,0:T(4,128)(2,1)}) %all-gather.3.cloned.1.call-update) | async-done | bytes 1310736 | tf_op jit(solution)/shard_map/all_gather | solution.py:46
  406.7 2.5 reshape.39
  409.2 7.7 %convolution_convert_fusion = bf16[2048,1280]{1,0:T(8,128)(2,1)} fusion(bf16[512,1280]{1,0:T(8,128)(2,1)S(1)} %reshape.39, f32[2048,512]{1,0:T(8,128)} %get-tuple-element.13, f32[2048]{0:T(1024)S(1)} %get-tuple-element.5, f32[2048]{0:T(1024)S(1)} %get-tuple-element.7), kind=kOutput, calls=%fused_computation | convolution fusion | flops 2690121728 | bytes 10764288 | tf_op jit(solution)/shard_map/dot_general | solution.py:47
  (3 shorter events, 0.1 us)
Async XLA Ops:
  6.5 1.3 copy-start
  15.3 8.4 %copy-start.1 = (f32[2048,512]{1,0:T(8,128)S(1)}, f32[2048,512]{1,0:T(8,128)}, u32[]{:S(2)}) copy-start(f32[2048,512]{1,0:T(8,128)} %get-tuple-element.13) | copy-start | bytes 12582916
  35.1 12.1 %copy-start.2 = (f32[1,1280]{1,0:T(1,128)S(1)}, f32[1,1280]{1,0:T(1,128)}, u32[]{:S(2)}) copy-start(f32[1,1280]{1,0:T(1,128)} %param.7) | copy-start | bytes 15364
  35.1 49.7 %all-to-all-start = ((f32[128,4,1282]{2,1,0:T(4,128)}), f32[128,4,1282]{2,1,0:T(4,128)}, u32[]{:S(2)}, u32[]{:S(2)}) async-start(f32[128,4,1282]{2,1,0:T(4,128)} %concatenate.13), calls=%async_computation | async-start | bytes 5767168 | tf_op jit(solution)/shard_map/all_to_all | solution.py:11
  47.0 359.7 %all-gather.3.cloned.1.call-start = ((), (), s32[]{:S(2)}) async-start(), calls=%async_computation.1 | async-start | bytes 1320960 | tf_op jit(solution)/shard_map/all_gather | solution.py:46
Sparse Core Ops, SparseCore 0:
  107.9 298.7 all-gather.2
where the time goes:
time: 424 us
  waiting for transfers between devices  336 us (79%)
  matrix products  30.5 us (7%)
  local copies, waits for them, and re-layouts  27.3 us (6%)
  between operations  13.5 us (3%)
  starting transfers between devices  12.1 us (3%)
    all_gather x1, waiting for transfers between devices, on_device(): gathered = lax.all_gather(expert_out, ('seq', 'grp'), axis=0, tiled=True)  299 us
    all_to_all x1, waiting for transfers between devices, in_one_piece(): lax.all_to_all(both, axis, split_axis=split_dim, concat_axis=concat_dim,...  37.5 us
    all_to_all x1, starting transfers between devices, in_one_piece(): lax.all_to_all(both, axis, split_axis=split_dim, concat_axis=concat_dim,...  11.9 us
    concatenate x4, local copies, waits for them, and re-layouts, in_one_piece(): both = jnp.concatenate(columns, axis=along)  10.2 us
  transfers between devices with their start and end apart: 2, of which 2 were waited for; matrix products, arithmetic and copies ran while one was open for 0% of the time, Pallas kernels for 0%

commit v1 on v0

--- a/solution.py
+++ b/solution.py
@@ -2,6 +2,13 @@
 import jax.numpy as jnp
 from jax import lax
 from jax.sharding import PartitionSpec as P
+
+
+def swapped_in(value, name, dim):
+    size = lax.axis_size(name)
+    shards = jnp.stack([value for _ in range(size)])
+    shards = lax.all_to_all(shards, name, split_axis=0, concat_axis=0)
+    return jnp.concatenate(shards, axis=dim)
 
 
 def in_one_piece(arrays, axis, split_dim, concat_dim, along):
@@ -43,7 +50,7 @@
     row_top = jnp.max(logits, axis=1, keepdims=True)
     row_exp = jnp.exp(logits - row_top)
     combine = (row_exp / jnp.sum(row_exp, axis=1, keepdims=True)).astype(jnp.bfloat16)
-    gathered = lax.all_gather(expert_out, ("seq", "grp"), axis=0, tiled=True)
+    gathered = swapped_in(expert_out, ("seq", "grp"), 0)
     mixed = jnp.dot(combine, gathered, preferred_element_type=jnp.float32)
     return mixed.astype(jnp.bfloat16)
 

time: 424 us -> 137 us (0.32)
  waiting for transfers between devices: 336 us -> 37.7 us
  blocking collectives: 0 us -> 25.7 us
  between operations: 13.5 us -> 0.09 us
    all_gather x1 -> x0, waiting for transfers between devices: 299 us -> none  [on_device(): gathered = lax.all_gather(expert_out, ('seq', 'grp'), axis=0, tiled=True)]
    all_to_all x0 -> x1, blocking collectives: none -> 25.7 us  [swapped_in(): shards = lax.all_to_all(shards, name, split_axis=0, concat_axis=0)]
  transfers between devices with their start and end apart: 2 -> 1, of which waited for: 2 -> 1; matrix products, arithmetic and copies ran while one was open for 0% -> 0% of each run, Pallas kernels for 0% -> 0%
where the time goes in v1:
time: 137 us; the launch traced here: 136 us
  waiting for transfers between devices  37.7 us (28%)
  matrix products  30.3 us (22%)
  local copies, waits for them, and re-layouts  26.3 us (19%)
  blocking collectives  25.7 us (19%)
  starting transfers between devices  11.9 us (9%)
  other arithmetic  4.03 us (3%)
    all_to_all x1, waiting for transfers between devices, in_one_piece(): lax.all_to_all(both, axis, split_axis=split_dim, concat_axis=concat_dim,...  37.7 us
    all_to_all x1, blocking collectives, swapped_in(): shards = lax.all_to_all(shards, name, split_axis=0, concat_axis=0)  25.7 us
    all_to_all x1, starting transfers between devices, in_one_piece(): lax.all_to_all(both, axis, split_axis=split_dim, concat_axis=concat_dim,...  11.9 us
    concatenate x4, local copies, waits for them, and re-layouts, in_one_piece(): both = jnp.concatenate(columns, axis=along)  10.2 us
    dot_general x1, matrix products, on_device(): lax.dot_general(weights, tokens, dims, preferred_element_type=jnp.float32)  8.36 us
    dot_general x1, matrix products, on_device(): mixed = jnp.dot(combine, gathered, preferred_element_type=jnp.float32)  8.12 us
    dot_general x1, matrix products, on_device(): logits = jnp.dot(tokens, slot_keys, preferred_element_type=jnp.float32)  7.07 us
    dot_general x1, matrix products, on_device(): jnp.dot(hidden, w_out[0], preferred_element_type=jnp.float32)  6.7 us
  transfers between devices with their start and end apart: 1, of which 1 were waited for; matrix products, arithmetic and copies ran while one was open for 0% of the time, Pallas kernels for 0%

profile of v1, /device:TPU:1, one launch (start us, length us, event | category | flops | bytes accessed | tf_op | source)
XLA Modules:
  0.0 136.0 jit_solution(12681431314428755300)
XLA Ops:
  0.0 0.0 copy-start
  0.0 1.3 copy-done
  1.3 7.1 %fusion.41 = (f32[2048]{0:T(1024)S(1)}, f32[512]{0:T(512)S(1)}, f32[2048,512]{1,0:T(8,128)}) fusion(bf16[2048,1280]{1,0:T(8,128)(2,1)} %param.5, bf16[1280,512]{1,0:T(8,128)(2,1)S(1)} %copy-done), kind=kOutput, calls=%fused_computation.41 | convolution fusion | flops 2686449152 | bytes 10758144 | tf_op jit(solution)/shard_map/dot_general | solution.py:31
  8.4 0.3 concatenate.14
  8.7 0.0 copy-start.1
  8.7 8.4 %fusion.10 = f32[512,1280]{1,0:T(8,128)} fusion(bf16[2048,1280]{1,0:T(8,128)(2,1)} %param.5, f32[2048,512]{1,0:T(8,128)} %get-tuple-element.13, f32[512]{0:T(512)S(1)} %get-tuple-element.8), kind=kOutput, calls=%fused_computation.13 | convolution fusion | flops 2686451712 | bytes 12060672 | tf_op jit(solution)/shard_map/dot_general | solution.py:38
  17.1 0.0 copy-done.1
  17.1 1.6 %fusion.4 = (f32[2048]{0:T(1024)S(1)}, f32[512]{0:T(512)S(1)}) fusion(f32[2048,512]{1,0:T(8,128)S(1)} %copy-done.1, f32[2048]{0:T(1024)S(1)} %get-tuple-element.7, f32[512]{0:T(512)S(1)} %get-tuple-element.8), kind=kLoop, calls=%fused_computation.8 | loop fusion | flops 4191744 | bytes 4214784 | tf_op jit(solution)/shard_map/reduce_sum | solution.py:52
  18.7 0.3 concatenate.15
  19.0 3.9 %concatenate.10 = f32[128,4,1280]{2,1,0:T(4,128)} reshape(f32[512,1280]{1,0:T(8,128)} %fusion.10) | data formatting | bytes 5242880 | tf_op jit(solution)/shard_map/concatenate | solution.py:16
  23.0 5.6 %concatenate.13 = f32[128,4,1282]{2,1,0:T(4,128)} concatenate(f32[128,4,1280]{2,1,0:T(4,128)} %concatenate.10, f32[128,4,1]{2,1,0:T(4,128)S(1)} %concatenate.14, f32[128,4,1]{2,1,0:T(4,128)S(1)} %concatenate.15), dimensions={2} | concatenate | bytes 5251072 | tf_op jit(solution)/shard_map/concatenate | solution.py:16
  28.6 0.0 copy-start.2
  28.6 11.9 %all-to-all-start = ((f32[128,4,1282]{2,1,0:T(4,128)}), f32[128,4,1282]{2,1,0:T(4,128)}, u32[]{:S(2)}, u32[]{:S(2)}) async-start(f32[128,4,1282]{2,1,0:T(4,128)} %concatenate.13), calls=%async_computation | async-start | bytes 5767168 | tf_op jit(solution)/shard_map/all_to_all | solution.py:18
  40.5 0.0 copy-done.2
  40.5 37.7 %all-to-all-done = f32[128,4,1282]{2,1,0:T(4,128)} async-done(((f32[128,4,1282]{2,1,0:T(4,128)}), f32[128,4,1282]{2,1,0:T(4,128)}, u32[]{:S(2)}, u32[]{:S(2)}) %all-to-all-start) | async-done | bytes 2625568 | tf_op jit(solution)/shard_map/all_to_all | solution.py:18
  78.2 4.4 %all_to_all.10 = f32[512,1282]{1,0:T(8,128)} reshape(f32[128,4,1282]{2,1,0:T(4,128)} %all-to-all-done) | data formatting | bytes 5251072 | tf_op jit(solution)/shard_map/all_to_all | solution.py:18
  82.6 1.3 slice_reduce_fusion
  84.0 3.4 %slice.12 = f32[512,1280]{1,0:T(8,128)} slice(f32[512,1282]{1,0:T(8,128)} %all_to_all.10), slice={[0:512], [0:1280]} | slice | bytes 5242880 | tf_op jit(solution)/shard_map/slice | solution.py:23
  87.4 3.9 %reshape.42 = f32[128,4,1280]{2,1,0:T(4,128)} reshape(f32[512,1280]{1,0:T(8,128)} %slice.12) | data formatting | bytes 5242880 | tf_op jit(solution)/shard_map/reshape | solution.py:42
  91.3 0.1 reshape_reshape.7
  91.4 0.1 reshape_reshape.6
  91.6 2.3 %multiply_reduce_fusion = f32[4,1280]{1,0:T(4,128)S(1)} fusion(f32[128,4,1280]{2,1,0:T(4,128)} %reshape.42, f32[128,4]{1,0:T(8,128)S(1)} %get-tuple-element.12), kind=kLoop, calls=%fused_computation.11 | loop fusion | flops 1305600 | bytes 2643968 | tf_op jit(solution)/shard_map/reduce_sum | solution.py:42
  93.9 6.7 %fusion.7 = bf16[4,1280]{1,0:T(4,128)(2,1)S(1)} fusion(bf16[1,2560,1280]{2,1,0:T(8,128)(2,1)} %param.9, bf16[1,1280,2560]{2,1,0:T(8,128)(2,1)} %param.8, f32[4,1280]{1,0:T(4,128)S(1)} %multiply_reduce_fusion, f32[1280]{0:T(1024)S(1)} %reduce.2, f32[4]{0:T(128)S(1)} %get-tuple-element.11), kind=kOutput, calls=%fused_computation.12 | convolution fusion | flops 52541440 | bytes 13143056 | tf_op jit(solution)/shard_map/dot_general | solution.py:49
  100.6 0.3 stack.2
  101.0 25.7 %all_to_all.14 = bf16[128,4,1280]{2,1,0:T(4,128)(2,1)S(1)} all-to-all(bf16[128,4,1280]{2,1,0:T(4,128)(2,1)S(1)} %stack.2), channel_id=1, replica_groups=mesh['seq'=16,'grp'=8] {'seq','grp'}, dimensions={0} | all-to-all | bytes 2621440 | tf_op jit(solution)/shard_map/all_to_all | solution.py:10
  126.7 1.2 reshape.43
  127.9 8.1 %convolution_convert_fusion = bf16[2048,1280]{1,0:T(8,128)(2,1)} fusion(bf16[512,1280]{1,0:T(8,128)(2,1)} %reshape.43, f32[2048,512]{1,0:T(8,128)} %get-tuple-element.13, f32[2048]{0:T(1024)S(1)} %get-tuple-element.5, f32[2048]{0:T(1024)S(1)} %get-tuple-element.7), kind=kOutput, calls=%fused_computation | convolution fusion | flops 2690121728 | bytes 10764288 | tf_op jit(solution)/shard_map/dot_general | solution.py:54
  (3 shorter events, 0.1 us)
Async XLA Ops:
  0.0 1.3 copy-start
  8.7 8.4 %copy-start.1 = (f32[2048,512]{1,0:T(8,128)S(1)}, f32[2048,512]{1,0:T(8,128)}, u32[]{:S(2)}) copy-start(f32[2048,512]{1,0:T(8,128)} %get-tuple-element.13) | copy-start | bytes 12582916
  28.6 11.9 %copy-start.2 = (f32[1,1280]{1,0:T(1,128)S(1)}, f32[1,1280]{1,0:T(1,128)}, u32[]{:S(2)}) copy-start(f32[1,1280]{1,0:T(1,128)} %param.7) | copy-start | bytes 15364
  28.6 49.6 %all-to-all-start = ((f32[128,4,1282]{2,1,0:T(4,128)}), f32[128,4,1282]{2,1,0:T(4,128)}, u32[]{:S(2)}, u32[]{:S(2)}) async-start(f32[128,4,1282]{2,1,0:T(4,128)} %concatenate.13), calls=%async_computation | async-start | bytes 5767168 | tf_op jit(solution)/shard_map/all_to_all | solution.py:18
